TPU v7x, 256 devices: a whole 4x4x8 slice. The times are simulated.
256 devices in a mesh: dp: 4 (over y), tensor: 64 (over x, z, core).
Axes of the slice: x: 4, y: 4, z: 8, core: 2. Of those that a mesh axis runs over, the one named last changes fastest.
Arguments:
- tokens: bfloat16 [4, 8192, 1536], P('dp', 'tensor'), may hold values from -6 to 6
- attn_gain: float32 [1536], replicated, may hold values from 0.1 to 1.9
- qkv_weight: bfloat16 [1536, 2560], P(None, 'dp'), may hold values from -0.25 to 0.25
- out_weight: bfloat16 [1536, 1536], P('dp'), may hold values from -0.15625 to 0.15625
- prefix_cache: bfloat16 [4, 512, 2, 512], P('dp', 'tensor'), may hold values from -640 to 640
- lengths: int32 [4, 256], P('dp'), may hold values from 1 to 384, 8192 in all within a row
- ffn_gain: float32 [1536], replicated, may hold values from 0.1 to 1.9
- expert_ids: int32 [4, 8192, 8], P('dp', 'tensor'), may hold values from 0 to 31, all different within a row; in each aligned block of 128 rows (0 to 127, 128 to 255, ..., all dimensions but the last counted through in order) at most 40 rows name the same one
- gate_weights: float32 [4, 8192, 8], P('dp', 'tensor'), may hold values from 0.05 to 0.5
- expert_in: bfloat16 [64, 1536, 512], P('tensor'), may hold values from -0.15625 to 0.15625
- expert_out: bfloat16 [64, 256, 1536], P('tensor'), may hold values from -0.25 to 0.25
Outputs:
- hidden_state: bfloat16 [4, 8192, 1536], P('dp', 'tensor')
- mixed: bfloat16 [4, 8192, 1536], P('dp', 'tensor')
Inputs may be any that keep to these rules, and one draw needn't show every extreme that they name: `lengths`: each group's 256 requests fill its 8192 suffix positions in order, and the longest holds exactly 384 tokens. `expert_ids`: each token names 8 different experts; among the 128 tokens of one device no expert is named more than 40 times, a bound that some block reaches.
All inputs are finite; a program needn't handle non-finite values.
Results may differ from a plain program's by a relative error of at most 0.014.
The roundings to bfloat16 on the way count: a program that leaves them out, or rounds other values in their place, can miss the bound.
Values may be sent and summed in bfloat16 or wider, within the bound.
No kernel may reach another device: no remote copies, remote signals or barrier semaphores. Data moves between devices by JAX's collectives and lax.ppermute only.
A program may use at most 128 MiB of HBM per device.

v0:
```python
import jax
import jax.numpy as jnp
from jax import lax
from jax.sharding import PartitionSpec as P

HEADS = 24
KV_HEADS = 8
HEAD_DIM = 64
EXPERTS = 32
TOPK = 8
SHIFTS = 2
CAP = 40
EPS = 1e-06
THETA = 10000.0


def from_behind(value, axis, steps):
    count = lax.axis_size(axis)
    first, last = (max(0, -steps), min(count, count - steps))
    return lax.ppermute(value, axis, [(source, source + steps) for source in range(first, last)])


def rms_norm(x, gain):
    values = x.astype(jnp.float32)
    mean_sq = jnp.mean(values * values, axis=-1, keepdims=True)
    return (values * lax.rsqrt(mean_sq + EPS) * gain).astype(jnp.bfloat16)


def rotary(x, positions):
    half = x.shape[-1] // 2
    freqs = THETA ** (-jnp.arange(half, dtype=jnp.float32) * 2.0 / x.shape[-1])
    angles = positions.astype(jnp.float32)[:, None] * freqs[None, :]
    cosine = jnp.concatenate([jnp.cos(angles), jnp.cos(angles)], axis=-1)[:, None, :]
    sine = jnp.concatenate([jnp.sin(angles), jnp.sin(angles)], axis=-1)[:, None, :]
    turned = jnp.concatenate([-x[..., half:], x[..., :half]], axis=-1)
    return x * cosine + turned * sine


def request_info(index, lengths):
    ends = jnp.cumsum(lengths, dtype=jnp.int32)
    before = ends[None, :] <= index[:, None]
    segment = jnp.sum(before.astype(jnp.int32), axis=1, dtype=jnp.int32)
    start = jnp.sum(jnp.where(before, lengths[None, :], 0), axis=1, dtype=jnp.int32)
    return (segment, index - start)


def merge_block(carry, scores, values, visible):
    best, total, acc = carry
    if visible is not None:
        scores = jnp.where(visible, scores, -1e30)
    newest = jnp.maximum(best, jnp.max(scores, axis=-1))
    probs = jnp.exp(scores - newest[..., None])
    if visible is not None:
        probs = jnp.where(visible, probs, 0.0)
    decay = jnp.exp(best - newest)
    total = total * decay + jnp.sum(probs, axis=-1)
    acc = acc * decay[..., None] + jnp.einsum(
        "tgrn,ngd->tgrd", probs.astype(jnp.bfloat16), values, preferred_element_type=jnp.float32
    )
    return (newest, total, acc)


def shards(
    tokens,
    attn_gain,
    qkv_weight,
    out_weight,
    prefix_cache,
    lengths,
    ffn_gain,
    expert_ids,
    gate_weights,
    expert_in,
    expert_out,
):
    rows = tokens.shape[1]
    model = tokens.shape[2]
    head_cols = HEADS * HEAD_DIM
    kv_cols = KV_HEADS * HEAD_DIM
    ratio = HEADS // KV_HEADS
    scale = 1.0 / HEAD_DIM**0.5
    lanes = lax.axis_size("tensor")
    prefix_len = prefix_cache.shape[1] * lanes
    own_lengths = lengths[0]
    inputs = tokens[0]
    normed = rms_norm(inputs, attn_gain)
    full_qkv, full_out = (
        lax.all_gather(qkv_weight, "dp", axis=1, tiled=True),
        lax.all_gather(out_weight, "dp", axis=0, tiled=True),
    )
    qkv = jnp.dot(normed, full_qkv, preferred_element_type=jnp.float32).astype(jnp.bfloat16)
    lane = lax.axis_index("tensor")
    q_index = lane * rows + jnp.arange(rows, dtype=jnp.int32)
    q_segment, offset = request_info(q_index, own_lengths)
    positions = prefix_len + offset
    query = rotary(
        qkv[:, :head_cols].astype(jnp.float32).reshape(rows, HEADS, HEAD_DIM), positions
    ).astype(jnp.bfloat16)
    query = query.reshape(rows, KV_HEADS, ratio, HEAD_DIM)
    keys = rotary(
        qkv[:, head_cols : head_cols + kv_cols]
        .astype(jnp.float32)
        .reshape(rows, KV_HEADS, HEAD_DIM),
        positions,
    ).astype(jnp.bfloat16)
    local_pairs = jnp.stack([keys.reshape(rows, kv_cols), qkv[:, head_cols + kv_cols :]], axis=1)
    start_carry = (
        jnp.full((rows, KV_HEADS, ratio), -1e30, jnp.float32),
        jnp.zeros((rows, KV_HEADS, ratio), jnp.float32),
        jnp.zeros((rows, KV_HEADS, ratio, HEAD_DIM), jnp.float32),
    )
    piece = lax.all_gather(prefix_cache[0], "tensor", axis=0, tiled=True)
    count = piece.shape[0]
    cached_keys = piece[:, 0].reshape(count, KV_HEADS, HEAD_DIM)
    cached_values = piece[:, 1].reshape(count, KV_HEADS, HEAD_DIM)
    scores = (
        jnp.einsum("tgrd,ngd->tgrn", query, cached_keys, preferred_element_type=jnp.float32) * scale
    )
    carry = merge_block(start_carry, scores, cached_values, None)
    window = local_pairs[None]
    for bit in range(SHIFTS):
        earlier = from_behind(window, "tensor", 2**bit)
        window = jnp.concatenate([window, earlier], axis=0)
    depth = window.shape[0]
    k_index = (
        (lane - jnp.arange(depth, dtype=jnp.int32))[:, None] * rows
        + jnp.arange(rows, dtype=jnp.int32)[None, :]
    ).reshape(-1)
    k_segment, unused = request_info(k_index, own_lengths)
    visible = (
        (k_index[None, :] >= 0)
        & (k_index[None, :] <= q_index[:, None])
        & (k_segment[None, :] == q_segment[:, None])
    )
    suffix_pairs = window.reshape(depth * rows, 2, kv_cols)
    suffix_keys = suffix_pairs[:, 0].reshape(depth * rows, KV_HEADS, HEAD_DIM)
    suffix_values = suffix_pairs[:, 1].reshape(depth * rows, KV_HEADS, HEAD_DIM)
    scores = (
        jnp.einsum("tgrd,ngd->tgrn", query, suffix_keys, preferred_element_type=jnp.float32) * scale
    )
    best, total, acc = merge_block(carry, scores, suffix_values, visible[:, None, None, :])
    attended = (acc / total[..., None]).astype(jnp.bfloat16).reshape(rows, head_cols)
    projected = jnp.dot(attended, full_out, preferred_element_type=jnp.float32)
    hidden_state = (inputs.astype(jnp.float32) + projected).astype(jnp.bfloat16)
    moe_input = rms_norm(hidden_state, ffn_gain)
    total_units = expert_in.shape[0] * lanes
    parts = total_units // EXPERTS
    unit_ff = expert_in.shape[2] // 2
    flat_ids = expert_ids[0].reshape(-1)
    onehot = (flat_ids[:, None] == jnp.arange(EXPERTS, dtype=jnp.int32)[None, :]).astype(jnp.int32)
    earlier_count = jnp.cumsum(onehot, axis=0, dtype=jnp.int32) - onehot
    slots = jnp.sum(earlier_count * onehot, axis=1, dtype=jnp.int32)
    unit_ids = flat_ids[:, None] * parts + jnp.arange(parts, dtype=jnp.int32)[None, :]
    target = (unit_ids * CAP + slots[:, None]).reshape(-1)
    row_of = jnp.repeat(jnp.arange(rows, dtype=jnp.int32), TOPK * parts)
    source = jnp.full((total_units * CAP,), rows, jnp.int32).at[target].set(row_of)
    padded_input = jnp.concatenate([moe_input, jnp.zeros((1, model), jnp.bfloat16)], axis=0)
    outgoing = padded_input[source]
    arrived = lax.all_to_all(
        outgoing.reshape(total_units, CAP, model), "tensor", split_axis=0, concat_axis=1, tiled=True
    )
    inner = jnp.einsum("erd,edf->erf", arrived, expert_in, preferred_element_type=jnp.float32)
    activated = (jax.nn.silu(inner[..., :unit_ff]) * inner[..., unit_ff:]).astype(jnp.bfloat16)
    produced = jnp.einsum(
        "erf,efd->erd", activated, expert_out, preferred_element_type=jnp.float32
    ).astype(jnp.bfloat16)
    returned = lax.all_to_all(produced, "tensor", split_axis=1, concat_axis=0, tiled=True)
    picked = returned.reshape(total_units * CAP, model)[target].reshape(rows, TOPK, parts, model)
    combined = jnp.einsum("tk,tksd->td", gate_weights[0], picked.astype(jnp.float32))
    mixed = (hidden_state.astype(jnp.float32) + combined).astype(jnp.bfloat16)
    return (hidden_state[None], mixed[None])


def solution(mesh):
    in_specs = (
        P("dp", "tensor", None),
        P(),
        P(None, "dp"),
        P("dp", None),
        P("dp", "tensor", None, None),
        P("dp", None),
        P(),
        P("dp", "tensor", None),
        P("dp", "tensor", None),
        P("tensor", None, None),
        P("tensor", None, None),
    )
    out_specs = (P("dp", "tensor", None), P("dp", "tensor", None))
    return jax.shard_map(shards, mesh=mesh, in_specs=in_specs, out_specs=out_specs, check_vma=False)
```

profile of v0, /device:TPU:1, one launch (start us, length us, event | category | flops | bytes accessed | tf_op | source)
XLA Modules:
  0.0 881.9 jit_solution(11526907995774648510)
XLA Ops:
  14.2 9.0 %reduce-window.19 = s32[32,8,128]{2,1,0:T(8,128)S(1)} reduce-window(s32[32,8,128]{2,1,0:T(8,128)S(1)} %fusion.61, s32[]{:T(128)} %constant.24.clone.1), window={size=1x1x128 pad=0_0x0_0x127_0}, to_apply=%region_11.12 | reduce-window | flops 4161536 | bytes 262148 | tf_op jit(solution)/shard_map/reduce-window.2
  24.5 8.1 scatter_custom_fusion
  34.4 57.4 %all-gather.9.cloned.1.call-done = bf16[1,512,2,512]{3,2,0,1:T(2,128)(2,1)} async-done(((bf16[1,8,2,512]{3,2,0,1:T(2,128)(2,1)}), bf16[1,512,2,512]{3,2,0,1:T(2,128)(2,1)}) %all-gather.9.cloned.1.call-update) | async-done | bytes 1048592 | tf_op jit(solution)/shard_map/all_gather | solution.py:112
  91.8 4.2 fusion.70
  96.0 3.5 copy.73
  99.5 3.5 copy.74
  103.0 69.1 %all-gather.5.cloned.1.call-done = bf16[1536,2560]{1,0:T(8,128)(2,1)} async-done(((bf16[1536,640]{1,0:T(8,128)(2,1)}), bf16[1536,2560]{1,0:T(8,128)(2,1)}) %all-gather.5.cloned.1.call-update) | async-done | bytes 7864336 | tf_op jit(solution)/shard_map/all_gather | solution.py:88
  172.1 4.5 convolution_convert_fusion.1
  178.5 3.9 collective-permute-start
  182.9 3.2 collective-permute-done
  187.2 3.7 collective-permute-start.1
  191.8 4.8 bitcast_reduce_fusion
  196.6 3.7 collective-permute-done.1
  203.8 2.1 copy.80
  207.0 3.7 fusion.3
  217.0 13.0 %all-gather.7.cloned.1.call-done = bf16[1536,1536]{1,0:T(8,128)(2,1)} async-done(((bf16[384,1536]{1,0:T(8,128)(2,1)}), bf16[1536,1536]{1,0:T(8,128)(2,1)}) %all-gather.7.cloned.1.call-update) | async-done | bytes 4718608 | tf_op jit(solution)/shard_map/all_gather | solution.py:89
  230.0 3.2 fusion.40
  233.5 9.5 %gather_fusion = bf16[2560,1536]{1,0:T(8,128)(2,1)} fusion(bf16[129,1536]{1,0:T(8,128)(2,1)S(1)} %concatenate.37, s32[3072]{0:T(1024)S(1)} %pad_clamp_fusion), kind=kCustom, calls=%fused_computation | custom fusion | bytes 15738880 | tf_op jit(solution)/shard_map/gather | solution.py:158
  243.0 185.6 %all_to_all.8 = bf16[64,40,1536]{2,1,0:T(8,128)(2,1)S(1)} all-to-all(bf16[64,40,1536]{2,1,0:T(8,128)(2,1)} %bitcast.167), channel_id=1, replica_groups=mesh['dp'=4,'tensor'=64] {'tensor'}, dimensions={0} | all-to-all | bytes 15728640 | tf_op jit(solution)/shard_map/all_to_all | solution.py:159
  428.6 4.2 convolution_bitcast_fusion
  432.8 2.3 fusion
  435.1 86.3 %copy.103 = bf16[1,2560,1536]{2,0,1:T(2,128)(2,1)} copy(bf16[1,2560,1536]{2,1,0:T(8,128)(2,1)S(1)} %fusion) | data formatting | bytes 15728640 | tf_op jit(solution)/shard_map/convert_element_type | solution.py:166
  522.0 51.5 %reduce.2 = bf16[2560,1536]{1,0:T(8,128)(2,1)} reduce(bf16[2560,1,1536]{2,1,0:T(2,128)(2,1)} %bitcast.165, bf16[]{:T(256)} %broadcast.284), dimensions={1}, to_apply=%bitcast.163.reduce_sub_computation | reduce | bytes 15728642
  573.5 17.7 %reshape.394 = bf16[64,2,30720]{2,1,0:T(2,128)(2,1)} reshape(bf16[2560,1536]{1,0:T(8,128)(2,1)} %reduce.2) | data formatting | bytes 15728640
  591.1 6.4 all-to-all-start.1
  597.8 174.3 %all-to-all-done.1 = bf16[64,2,30720]{2,1,0:T(2,128)(2,1)} async-done(((bf16[64,2,30720]{2,1,0:T(2,128)(2,1)}), bf16[64,2,30720]{2,1,0:T(2,128)(2,1)}, u32[]{:S(2)}, u32[]{:S(2)}) %all-to-all-start.1) | async-done | bytes 7864352 | tf_op jit(solution)/shard_map/all_to_all | solution.py:167
  772.1 38.0 %reshape.395 = bf16[2560,1,1536]{2,1,0:T(2,128)(2,1)} reshape(bf16[64,2,30720]{2,1,0:T(2,128)(2,1)} %all-to-all-done.1) | data formatting | bytes 15728640
  810.1 10.8 %copy.102 = bf16[1,2560,1536]{2,1,0:T(8,128)(2,1)} copy(bf16[1,2560,1536]{2,0,1:T(2,128)(2,1)} %bitcast.166) | data formatting | bytes 15728640
  820.9 17.5 %gather_fusion.1 = bf16[2048,1536]{1,0:T(8,128)(2,1)} fusion(bf16[2560,1536]{1,0:T(8,128)(2,1)} %bitcast.164, s32[2048]{0:T(1024)S(1)} %broadcast_clamp_fusion), kind=kCustom, calls=%fused_computation.1 | custom fusion | bytes 12591104 | tf_op jit(solution)/shard_map/gather | solution.py:168
  838.4 14.1 %reshape.358 = f32[128,8,2,1536]{3,2,1,0:T(2,128)} reshape(bf16[2048,1536]{1,0:T(8,128)(2,1)} %gather_fusion.1) | data formatting | bytes 18874368 | tf_op jit(solution)/shard_map/convert_element_type | solution.py:169
  852.6 18.9 %reduce_sum.89 = bf16[128,8,1536]{2,1,0:T(8,128)(2,1)} reduce(f32[128,8,2,1536]{3,2,1,0:T(2,128)} %reshape.358, f32[]{:T(128)} %constant.19.clone.1), dimensions={2}, to_apply=%region_15.16 | reduce | flops 1572864 | bytes 15728644 | tf_op jit(solution)/shard_map/tk,tksd->td/reduce_sum | solution.py:169
  871.4 2.8 fusion.72
  (107 shorter events, 26.7 us)
Async XLA Ops:
  7.2 421.4 %copy-start = (bf16[1,1536,512]{2,1,0:T(8,128)(2,1)S(1)}, bf16[1,1536,512]{2,1,0:T(8,128)(2,1)}, u32[]{:S(2)}) copy-start(bf16[1,1536,512]{2,1,0:T(8,128)(2,1)} %param.20) | copy-start | bytes 4718596
  7.2 84.6 %all-gather.9.cloned.1.call-start = ((), (), s32[]{:S(2)}) async-start(), calls=%async_computation.4 | async-start | bytes 1064960 | tf_op jit(solution)/shard_map/all_gather | solution.py:112
  7.9 164.2 %all-gather.5.cloned.1.call-start = ((), (), s32[]{:S(2)}) async-start(), calls=%async_computation.2 | async-start | bytes 9830400 | tf_op jit(solution)/shard_map/all_gather | solution.py:88
  8.7 163.5 %copy-start.2 = (bf16[1,128,1536]{2,1,0:T(8,128)(2,1)S(1)}, bf16[1,128,1536]{2,1,0:T(8,128)(2,1)}, u32[]{:S(2)}) copy-start(bf16[1,128,1536]{2,1,0:T(8,128)(2,1)} %param.11) | copy-start | bytes 1179652
  8.7 163.4 %copy-start.8 = (f32[1536]{0:T(1024)S(1)}, f32[1536]{0:T(1024)}, u32[]{:S(2)}) copy-start(f32[1536]{0:T(1024)} %param.12) | copy-start | bytes 18436
  8.7 221.3 %all-gather.7.cloned.1.call-start = ((), (), s32[]{:S(2)}) async-start(), calls=%async_computation.3 | async-start | bytes 5898240 | tf_op jit(solution)/shard_map/all_gather | solution.py:89
  24.4 8.2 copy-start.9
  34.2 68.8 %copy-start.7 = (f32[128,64]{0,1:T(8,128)}, f32[128,64]{0,1:T(8,128)S(1)}, u32[]{:S(2)}) copy-start(f32[128,64]{0,1:T(8,128)S(1)} %get-tuple-element.27) | copy-start | bytes 98308
  178.5 7.5 collective-permute-start
  187.2 13.1 %collective-permute-start.1 = (bf16[2,128,2,512]{3,1,2,0:T(8,128)(2,1)S(1)}, bf16[2,128,2,512]{3,1,2,0:T(8,128)(2,1)S(1)}, u32[]{:S(2)}, u32[]{:S(2)}) collective-permute-start(bf16[2,128,2,512]{3,1,2,0:T(8,128)(2,1)S(1)} %pad_maximum_fusion.1), channel_id=1, source_target_pairs={{0,2},{1,3},{2,4},{3,5},{4,6},{5,7},{6,8},{7,9},{8,10},{9,11},{10,... | collective-permute-start | bytes 1572872 | tf_op jit(solution)/shard_map/ppermute | solution.py:20
  191.8 14.1 %copy-start.4 = (pred[128,512]{0,1:T(8,128)(4,1)S(1)}, pred[128,512]{0,1:T(8,128)(4,1)}, u32[]{:S(2)}) copy-start(pred[128,512]{0,1:T(8,128)(4,1)} %compare_and_fusion) | copy-start | bytes 196612
  207.0 5.3 copy-start.6
  212.2 2.4 slice-start
  212.3 2.4 copy-start.5
  212.3 3.0 slice-start.1
  215.3 18.0 %copy-start.11 = (f32[1536]{0:T(1024)S(1)}, f32[1536]{0:T(1024)}, u32[]{:S(2)}) copy-start(f32[1536]{0:T(1024)} %param.17) | copy-start | bytes 18436
  233.2 641.1 %copy-start.3 = (bf16[128,1536]{1,0:T(8,128)(2,1)}, bf16[128,1536]{1,0:T(8,128)(2,1)S(1)}, u32[]{:S(2)}) copy-start(bf16[128,1536]{1,0:T(8,128)(2,1)S(1)} %get-tuple-element.26) | copy-start | bytes 1179652
  428.6 4.3 copy-start.13
  591.1 6.4 copy-start.12
  591.1 6.6 copy-start.10
  591.1 181.0 %all-to-all-start.1 = ((bf16[64,2,30720]{2,1,0:T(2,128)(2,1)}), bf16[64,2,30720]{2,1,0:T(2,128)(2,1)}, u32[]{:S(2)}, u32[]{:S(2)}) async-start(bf16[64,2,30720]{2,1,0:T(2,128)(2,1)} %reshape.394), calls=%async_computation.1 | async-start | bytes 15728640 | tf_op jit(solution)/shard_map/all_to_all | solution.py:167
  852.6 22.6 %copy-start.1 = (bf16[1,1536,512]{2,1,0:T(8,128)(2,1)S(1)}, bf16[1,1536,512]{2,1,0:T(8,128)(2,1)}, u32[]{:S(2)}) copy-start(bf16[1,1536,512]{2,1,0:T(8,128)(2,1)} %param.20) | copy-start | bytes 4718596
Sparse Core Ops, SparseCore 0:
  10.8 80.9 all-gather.8
  93.6 78.4 all-gather.4
  173.9 56.0 all-gather.6
where the time goes:
time: 890 us; the launch traced here: 882 us
  waiting for transfers between devices  323 us (36%)
  local copies, waits for them, and re-layouts  222 us (25%)
  blocking collectives  186 us (21%)
  other arithmetic  96.3 us (11%)
  matrix products  26.4 us (3%)
  between operations  14.5 us (2%)
  starting transfers between devices  14.1 us (2%)
    all_to_all x1, blocking collectives, shards(): lax.all_to_all(outgoing.reshape(total_units, CAP, model), 'tensor', split...  186 us
    all_to_all x1, waiting for transfers between devices, shards(): lax.all_to_all(produced, 'tensor', split_axis=1, concat_axis=0, tiled=True)  174 us
    convert_element_type x1, local copies, waits for them, and re-layouts, shards(): produced = jnp.einsum('erf,efd->erd', activated, expert_out, preferred_el...  86.3 us
    all_gather x1, waiting for transfers between devices, shards(): lax.all_gather(qkv_weight, 'dp', axis=1, tiled=True)  69.1 us
    unnamed x37, local copies, waits for them, and re-layouts  69.1 us
    all_gather x1, waiting for transfers between devices, shards(): piece = lax.all_gather(prefix_cache[0], 'tensor', axis=0, tiled=True)  57.4 us
    unnamed x2, other arithmetic  51.5 us
    reduce_sum x1, other arithmetic, shards(): jnp.einsum('tk,tksd->td', gate_weights[0], picked.astype(jnp.float32))  18.9 us
  transfers between devices with their start and end apart: 6, of which 6 were waited for; matrix products, arithmetic and copies ran while one was open for 7% of the time, Pallas kernels for 0%

commit v1 on v0

--- a/solution.py
+++ b/solution.py
@@ -1,3 +1,4 @@
+import functools
 import jax
 import jax.numpy as jnp
 from jax import lax
@@ -12,6 +13,34 @@
 CAP = 40
 EPS = 1e-06
 THETA = 10000.0
+
+
+def _raise_field(state, mesh_name):
+    a_next, tile_out, high = (
+        jax.lax.psum(1, mesh_name),
+        jax.lax.axis_index(mesh_name),
+        state.shape[1],
+    )
+    bank = [(it, (it + 1) % a_next) for it in range(a_next)]
+    all_blocks = [(it, (it - 1) % a_next) for it in range(a_next)]
+    piece_out = jnp.zeros((*state.shape[:1], a_next * high, *state.shape[2:]), state.dtype)
+    piece_out = lax.dynamic_update_slice_in_dim(piece_out, state, tile_out * high, axis=1)
+    big = a_next // 2
+    out_arr = response = state
+    for at in range(1, big + 1):
+        out_arr = jax.lax.ppermute(out_arr, mesh_name, bank)
+        piece_out = lax.dynamic_update_slice_in_dim(
+            piece_out, out_arr, (tile_out - at) % a_next * high, axis=1
+        )
+        if at < a_next - big:
+            response = jax.lax.ppermute(response, mesh_name, all_blocks)
+            piece_out = lax.dynamic_update_slice_in_dim(
+                piece_out, response, (tile_out + at) % a_next * high, axis=1
+            )
+    return piece_out
+
+
+_choose_screen = functools.partial(_raise_field, mesh_name="dp")
 
 
 def from_behind(value, axis, steps):
@@ -85,7 +114,7 @@
     inputs = tokens[0]
     normed = rms_norm(inputs, attn_gain)
     full_qkv, full_out = (
-        lax.all_gather(qkv_weight, "dp", axis=1, tiled=True),
+        _choose_screen(qkv_weight),
         lax.all_gather(out_weight, "dp", axis=0, tiled=True),
     )
     qkv = jnp.dot(normed, full_qkv, preferred_element_type=jnp.float32).astype(jnp.bfloat16)

time: 890 us -> 816 us (0.917)
  waiting for transfers between devices: 323 us -> 208 us
  local copies, waits for them, and re-layouts: 222 us -> 244 us
  other arithmetic: 96.3 us -> 107 us
    all_gather x1 -> x0, waiting for transfers between devices: 69.1 us -> none  [shards(): lax.all_gather(qkv_weight, 'dp', axis=1, tiled=True)]
    all_gather x1, waiting for transfers between devices: 57.4 us -> 19.8 us  [shards(): piece = lax.all_gather(prefix_cache[0], 'tensor', axis=0, tiled=True)]
    all_gather x1, waiting for transfers between devices: 13 us -> 0.02 us  [shards(): lax.all_gather(out_weight, 'dp', axis=0, tiled=True)]
    dynamic_update_slice x0 -> x4, local copies, waits for them, and re-layouts: none -> 11 us  [the longest x2 6.36 us: _raise_field(): lax.dynamic_update_slice_in_dim(piece_out, out_arr, (tile_out - at) % a_n...]
    unnamed x37 -> x43, local copies, waits for them, and re-layouts: 69.1 us -> 69.1 us
  transfers between devices with their start and end apart: 6 -> 8, of which waited for: 6 -> 5; matrix products, arithmetic and copies ran while one was open for 7% -> 12% of each run, Pallas kernels for 0% -> 0%
where the time goes in v1:
time: 816 us; the launch traced here: 805 us
  local copies, waits for them, and re-layouts  244 us (30%)
  waiting for transfers between devices  208 us (25%)
  blocking collectives  188 us (23%)
  other arithmetic  107 us (13%)
  matrix products  26.5 us (3%)
  starting transfers between devices  18.4 us (2%)
  between operations  14.7 us (2%)
    all_to_all x1, blocking collectives, shards(): lax.all_to_all(outgoing.reshape(total_units, CAP, model), 'tensor', split...  188 us
    all_to_all x1, waiting for transfers between devices, shards(): lax.all_to_all(produced, 'tensor', split_axis=1, concat_axis=0, tiled=True)  174 us
    convert_element_type x1, local copies, waits for them, and re-layouts, shards(): produced = jnp.einsum('erf,efd->erd', activated, expert_out, preferred_el...  86.3 us
    unnamed x43, local copies, waits for them, and re-layouts  69.1 us
    unnamed x2, other arithmetic  51.5 us
    all_gather x1, waiting for transfers between devices, shards(): piece = lax.all_gather(prefix_cache[0], 'tensor', axis=0, tiled=True)  19.8 us
    reduce_sum x1, other arithmetic, shards(): jnp.einsum('tk,tksd->td', gate_weights[0], picked.astype(jnp.float32))  18.9 us
    gather x1, local copies, waits for them, and re-layouts, shards(): returned.reshape(total_units * CAP, model)[target]  17.5 us
  transfers between devices with their start and end apart: 8, of which 5 were waited for; matrix products, arithmetic and copies ran while one was open for 12% of the time, Pallas kernels for 0%

profile of v1, /device:TPU:1, one launch (start us, length us, event | category | flops | bytes accessed | tf_op | source)
XLA Modules:
  0.0 805.0 jit_solution(10916416039320408288)
XLA Ops:
  14.6 9.0 %reduce-window.19 = s32[32,8,128]{2,1,0:T(8,128)S(1)} reduce-window(s32[32,8,128]{2,1,0:T(8,128)S(1)} %fusion.61, s32[]{:T(128)} %constant.38.clone.1), window={size=1x1x128 pad=0_0x0_0x127_0}, to_apply=%region_11.12 | reduce-window | flops 4161536 | bytes 262148 | tf_op jit(solution)/shard_map/reduce-window.2
  33.6 8.8 %scatter_custom_fusion = s32[2560]{0:T(1024)} fusion(s32[2048]{0:T(1024)} %bitcast.187, s32[2048]{0:T(1024)} %reshape.379, s32[]{:T(128)} %constant.86.clone.1), kind=kCustom, calls=%fused_computation.93 | custom fusion | bytes 10752 | tf_op jit(solution)/shard_map/scatter | solution.py:185
  47.1 5.4 collective-permute-done
  60.7 3.7 broadcast_in_dim.51
  65.9 3.1 constant_dynamic-update-slice_fusion.2
  68.9 3.1 constant_dynamic-update-slice_fusion.1
  72.0 19.8 %all-gather.6.cloned.1.call-done = bf16[1,512,2,512]{3,2,0,1:T(2,128)(2,1)} async-done(((bf16[1,8,2,512]{3,2,0,1:T(2,128)(2,1)}), bf16[1,512,2,512]{3,2,0,1:T(2,128)(2,1)}) %all-gather.6.cloned.1.call-update) | async-done | bytes 1048592 | tf_op jit(solution)/shard_map/all_gather | solution.py:141
  91.8 4.4 fusion.70
  96.2 3.5 copy.73
  99.7 3.5 copy.74
  103.3 3.3 constant_dynamic-update-slice_fusion
  106.6 4.5 convolution_convert_fusion.1
  116.1 3.2 collective-permute-done.3
  120.4 4.1 collective-permute-start.4
  125.4 4.8 bitcast_reduce_fusion
  130.2 4.1 collective-permute-done.4
  140.9 3.7 fusion.3
  150.8 3.2 fusion.40
  154.3 9.5 %gather_fusion = bf16[2560,1536]{1,0:T(8,128)(2,1)} fusion(bf16[129,1536]{1,0:T(8,128)(2,1)S(1)} %concatenate.37, s32[3072]{0:T(1024)S(1)} %pad_clamp_fusion), kind=kCustom, calls=%fused_computation | custom fusion | bytes 15738880 | tf_op jit(solution)/shard_map/gather | solution.py:187
  163.9 187.6 %all_to_all.8 = bf16[64,40,1536]{2,1,0:T(8,128)(2,1)S(1)} all-to-all(bf16[64,40,1536]{2,1,0:T(8,128)(2,1)} %bitcast.167), channel_id=1, replica_groups=mesh['dp'=4,'tensor'=64] {'tensor'}, dimensions={0} | all-to-all | bytes 15728640 | tf_op jit(solution)/shard_map/all_to_all | solution.py:188
  351.4 4.2 convolution_bitcast_fusion
  358.0 86.3 %copy.103 = bf16[1,2560,1536]{2,0,1:T(2,128)(2,1)} copy(bf16[1,2560,1536]{2,1,0:T(8,128)(2,1)S(1)} %fusion) | data formatting | bytes 15728640 | tf_op jit(solution)/shard_map/convert_element_type | solution.py:195
  444.8 51.5 %reduce.2 = bf16[2560,1536]{1,0:T(8,128)(2,1)} reduce(bf16[2560,1,1536]{2,1,0:T(2,128)(2,1)} %bitcast.165, bf16[]{:T(256)} %broadcast.287), dimensions={1}, to_apply=%bitcast.163.reduce_sub_computation | reduce | bytes 15728642
  496.3 17.7 %reshape.394 = bf16[64,2,30720]{2,1,0:T(2,128)(2,1)} reshape(bf16[2560,1536]{1,0:T(8,128)(2,1)} %reduce.2) | data formatting | bytes 15728640
  514.0 6.4 all-to-all-start.1
  520.6 174.3 %all-to-all-done.1 = bf16[64,2,30720]{2,1,0:T(2,128)(2,1)} async-done(((bf16[64,2,30720]{2,1,0:T(2,128)(2,1)}), bf16[64,2,30720]{2,1,0:T(2,128)(2,1)}, u32[]{:S(2)}, u32[]{:S(2)}) %all-to-all-start.1) | async-done | bytes 7864352 | tf_op jit(solution)/shard_map/all_to_all | solution.py:196
  694.9 38.0 %reshape.395 = bf16[2560,1,1536]{2,1,0:T(2,128)(2,1)} reshape(bf16[64,2,30720]{2,1,0:T(2,128)(2,1)} %all-to-all-done.1) | data formatting | bytes 15728640
  732.9 10.8 %copy.102 = bf16[1,2560,1536]{2,1,0:T(8,128)(2,1)} copy(bf16[1,2560,1536]{2,0,1:T(2,128)(2,1)} %bitcast.166) | data formatting | bytes 15728640
  743.7 17.5 %gather_fusion.1 = bf16[2048,1536]{1,0:T(8,128)(2,1)} fusion(bf16[2560,1536]{1,0:T(8,128)(2,1)} %bitcast.164, s32[2048]{0:T(1024)S(1)} %broadcast_clamp_fusion), kind=kCustom, calls=%fused_computation.1 | custom fusion | bytes 12591104 | tf_op jit(solution)/shard_map/gather | solution.py:197
  761.3 14.1 %reshape.358 = f32[128,8,2,1536]{3,2,1,0:T(2,128)} reshape(bf16[2048,1536]{1,0:T(8,128)(2,1)} %gather_fusion.1) | data formatting | bytes 18874368 | tf_op jit(solution)/shard_map/convert_element_type | solution.py:198
  775.4 18.9 %reduce_sum.89 = bf16[128,8,1536]{2,1,0:T(8,128)(2,1)} reduce(f32[128,8,2,1536]{3,2,1,0:T(2,128)} %reshape.358, f32[]{:T(128)} %constant.32.clone.1), dimensions={2}, to_apply=%region_15.16 | reduce | flops 1572864 | bytes 15728644 | tf_op jit(solution)/shard_map/tk,tksd->td/reduce_sum | solution.py:198
  794.3 2.8 fusion.72
  (121 shorter events, 55.4 us)
Async XLA Ops:
  7.2 344.3 %copy-start = (bf16[1,1536,512]{2,1,0:T(8,128)(2,1)S(1)}, bf16[1,1536,512]{2,1,0:T(8,128)(2,1)}, u32[]{:S(2)}) copy-start(bf16[1,1536,512]{2,1,0:T(8,128)(2,1)} %param.20) | copy-start | bytes 4718596
  7.2 84.6 %all-gather.6.cloned.1.call-start = ((), (), s32[]{:S(2)}) async-start(), calls=%async_computation.3 | async-start | bytes 1064960 | tf_op jit(solution)/shard_map/all_gather | solution.py:141
  7.9 142.9 %all-gather.4.cloned.1.call-start = ((), (), s32[]{:S(2)}) async-start(), calls=%async_computation.2 | async-start | bytes 5898240 | tf_op jit(solution)/shard_map/all_gather | solution.py:118
  8.0 44.6 %collective-permute-start = (bf16[1536,640]{1,0:T(8,128)(2,1)}, bf16[1536,640]{1,0:T(8,128)(2,1)}, u32[]{:S(2)}, u32[]{:S(2)}) collective-permute-start(bf16[1536,640]{1,0:T(8,128)(2,1)} %param.13), channel_id=1, source_target_pairs={{0,64},{64,128},{128,192},{192,0},{1,65},{65,129},{129,193},{193,1... | collective-permute-start | bytes 5898248 | tf_op jit(solution)/shard_map/ppermute | solution.py:31
  10.2 58.8 %collective-permute-start.1 = (bf16[1536,640]{1,0:T(8,128)(2,1)}, bf16[1536,640]{1,0:T(8,128)(2,1)}, u32[]{:S(2)}, u32[]{:S(2)}) collective-permute-start(bf16[1536,640]{1,0:T(8,128)(2,1)} %param.13), channel_id=1, source_target_pairs={{0,192},{64,0},{128,64},{192,128},{1,193},{65,1},{129,65},{193,129... | collective-permute-start | bytes 5898248 | tf_op jit(solution)/shard_map/ppermute | solution.py:36
  14.6 12.9 %copy-start.11 = (s32[256]{0:T(256)}, s32[256]{0:T(256)S(1)}, u32[]{:S(2)}) copy-start(s32[256]{0:T(256)S(1)} %add_bitcast_fusion.1) | copy-start | bytes 3076
  25.9 38.4 %copy-start.4 = (bf16[1536,640]{1,0:T(8,128)(2,1)S(1)}, bf16[1536,640]{1,0:T(8,128)(2,1)}, u32[]{:S(2)}) copy-start(bf16[1536,640]{1,0:T(8,128)(2,1)} %param.13) | copy-start | bytes 5898244
  25.9 1.5 copy-start.15
  52.5 50.7 %collective-permute-start.2 = (bf16[1536,640]{1,0:T(8,128)(2,1)}, bf16[1536,640]{1,0:T(8,128)(2,1)}, u32[]{:S(2)}, u32[]{:S(2)}) collective-permute-start(bf16[1536,640]{1,0:T(8,128)(2,1)} %collective-permute-done), channel_id=1, source_target_pairs={{0,64},{64,128},{128,192},{192,0},{1,65},{65,129},{129,193},{193,1... | collective-permute-start | bytes 5898248 | tf_op jit(solution)/shard_map/ppermute | solution.py:31
  72.0 34.5 %copy-start.2 = (bf16[1,128,1536]{2,1,0:T(8,128)(2,1)S(1)}, bf16[1,128,1536]{2,1,0:T(8,128)(2,1)}, u32[]{:S(2)}) copy-start(bf16[1,128,1536]{2,1,0:T(8,128)(2,1)} %param.11) | copy-start | bytes 1179652
  72.0 34.5 %copy-start.9 = (f32[1536]{0:T(1024)S(1)}, f32[1536]{0:T(1024)}, u32[]{:S(2)}) copy-start(f32[1536]{0:T(1024)} %param.12) | copy-start | bytes 18436
  72.0 34.5 %copy-start.14 = (f32[128]{0:T(128)S(1)}, f32[128]{0:T(128)}, u32[]{:S(2)}) copy-start(f32[128]{0:T(128)} %add_rsqrt_fusion.1) | copy-start | bytes 1540
  106.6 5.7 copy-start.5
  113.1 6.2 collective-permute-start.3
  120.4 13.9 %collective-permute-start.4 = (bf16[2,128,2,512]{3,1,2,0:T(8,128)(2,1)S(1)}, bf16[2,128,2,512]{3,1,2,0:T(8,128)(2,1)S(1)}, u32[]{:S(2)}, u32[]{:S(2)}) collective-permute-start(bf16[2,128,2,512]{3,1,2,0:T(8,128)(2,1)S(1)} %pad_maximum_fusion.1), channel_id=1, source_target_pairs={{0,2},{1,3},{2,4},{3,5},{4,6},{5,7},{6,8},{7,9},{8,10},{9,11},{10,... | collective-permute-start | bytes 1572872 | tf_op jit(solution)/shard_map/ppermute | solution.py:49
  125.4 14.5 %copy-start.6 = (pred[128,512]{0,1:T(8,128)(4,1)S(1)}, pred[128,512]{0,1:T(8,128)(4,1)}, u32[]{:S(2)}) copy-start(pred[128,512]{0,1:T(8,128)(4,1)} %compare_and_fusion) | copy-start | bytes 196612
  140.9 5.2 copy-start.8
  146.1 2.3 slice-start
  146.1 2.3 copy-start.7
  146.2 3.0 slice-start.1
  149.1 5.0 copy-start.12
  154.1 643.0 %copy-start.3 = (bf16[128,1536]{1,0:T(8,128)(2,1)}, bf16[128,1536]{1,0:T(8,128)(2,1)S(1)}, u32[]{:S(2)}) copy-start(bf16[128,1536]{1,0:T(8,128)(2,1)S(1)} %get-tuple-element.26) | copy-start | bytes 1179652
  351.4 4.3 copy-start.16
  514.0 6.4 copy-start.13
  514.0 6.6 copy-start.10
  514.0 180.9 %all-to-all-start.1 = ((bf16[64,2,30720]{2,1,0:T(2,128)(2,1)}), bf16[64,2,30720]{2,1,0:T(2,128)(2,1)}, u32[]{:S(2)}, u32[]{:S(2)}) async-start(bf16[64,2,30720]{2,1,0:T(2,128)(2,1)} %reshape.394), calls=%async_computation.1 | async-start | bytes 15728640 | tf_op jit(solution)/shard_map/all_to_all | solution.py:196
  775.4 22.6 %copy-start.1 = (bf16[1,1536,512]{2,1,0:T(8,128)(2,1)S(1)}, bf16[1,1536,512]{2,1,0:T(8,128)(2,1)}, u32[]{:S(2)}) copy-start(bf16[1,1536,512]{2,1,0:T(8,128)(2,1)} %param.20) | copy-start | bytes 4718596
Sparse Core Ops, SparseCore 0:
  10.8 81.0 all-gather.5
  93.6 52.3 all-gather.3
